TPU v7x, 32 devices: a whole 2x2x4 slice. The times are simulated.
32 devices in a mesh: dp: 2 (over core), ep: 16 (over z, y, x).
Axes of the slice: x: 2, y: 2, z: 4, core: 2. Of those that a mesh axis runs over, the one named last changes fastest.
Arguments:
- latent_cache: bfloat16 [16, 4, 512, 576], P('ep', 'dp'), may hold values from -6 to 6
- lengths: int32 [16, 4], P(None, 'dp'), may hold values from 2 to 512
- new_home: int32 [16, 4], P(None, 'dp'), may hold values from 0 to 15, as said below
- queries: bfloat16 [2, 16, 4, 128, 576], P(None, 'ep', 'dp'), may hold values from -32 to 32
- new_latent: bfloat16 [2, 16, 4, 576], P(None, 'ep', 'dp'), may hold values from -6 to 6
- hidden: bfloat16 [2, 16, 4, 3584], P(None, 'ep', 'dp'), may hold values from -6 to 6
- routes: int32 [2, 16, 4, 8], P(None, 'ep', 'dp'), may hold values from 0 to 15, all different within a row; in each aligned block of 4 rows (0 to 3, 4 to 7, ..., all dimensions but the last counted through in order) at most 4 rows name the same one
- route_logits: bfloat16 [2, 16, 4, 8], P(None, 'ep', 'dp'), may hold values from -8 to 8
- w_gate: bfloat16 [16, 3584, 1024], P('ep', None, 'dp'), may hold values from -0.09375 to 0.09375
- w_up: bfloat16 [16, 3584, 1024], P('ep', None, 'dp'), may hold values from -0.09375 to 0.09375
- w_down: bfloat16 [16, 1024, 3584], P('ep', 'dp'), may hold values from -0.1875 to 0.1875
Outputs:
- attended: bfloat16 [2, 16, 4, 128, 512], P(None, 'ep', 'dp')
- moe_out: bfloat16 [2, 16, 4, 3584], P(None, 'ep', 'dp')
Inputs may be any that keep to these rules, and one draw needn't show every extreme that they name: `routes`: in each step, the 4 requests of one ep index name any one expert in at most 4 of their choices, and this bound is reached. For each request index c, new_home[., c] exchanges exactly two ep indices and leaves every other one in place, so new_home[new_home[e, c], c] == e; the two indices lie 16 // 2 apart for even c and 1 apart (modulo 16) for odd c.
All inputs are finite; a program needn't handle non-finite values.
Results may differ from a plain program's by a relative error of at most 0.0057.
Values may be sent and summed in bfloat16 or wider, within the bound.
A program may use at most 128 MiB of HBM per device.

v0:
```python
import functools

import jax
import jax.numpy as jnp
from jax import lax
from jax.experimental import pallas as pl
from jax.experimental.pallas import tpu as pltpu
from jax.sharding import PartitionSpec as P


KV_RANK = 512
HEAD_QK = 192
LANES = 128
MESH = pl.DeviceIdType.MESH
GATHER_CHUNKS = 2
RETURN_CHUNKS = 4


def ladder_kernel(
    plan,
    lengths_ref,
    homes_ref,
    fresh_ref,
    hidden_ref,
    routes_ref,
    logits_ref,
    cache_hbm,
    query_hbm,
    gate_hbm,
    up_hbm,
    down_hbm,
    attended_hbm,
    moe_ref,
    column,
    tokens,
    query,
    cache,
    w_gate,
    w_up,
    w_down,
    served,
    far,
    near,
    onward,
    moved,
    own_part,
    pair_send,
    pair_recv,
    chip_part,
    chip_send,
    first_recv,
    second_keep,
    second_send,
    second_recv,
    line_part,
    line_send,
    line_recv,
    load_sem,
    send_sem,
    recv_sem,
):
    ranks, line = plan["ranks"], plan["line"]
    steps, requests = hidden_ref.shape[0], hidden_ref.shape[2]
    own_rows = steps * requests
    lat = cache.shape[1]
    heads = query.shape[-1]
    width = hidden_ref.shape[-1]
    blocks = width // LANES
    layers = blocks + 1
    half = 4
    core = lax.axis_index("dp")
    rank = lax.axis_index("ep")
    side, up, place = lax.rem(rank, 2), lax.rem(lax.div(rank, 2), 2), lax.div(rank, 4)
    cell = lax.rem(rank, 4)
    across_side, across_up = rank + 1 - 2 * side, rank + 2 - 4 * up
    first = across_up * (1 - core) + across_side * core
    second = across_side * (1 - core) + across_up * core
    first_cell, corner = lax.rem(first, 4), 3 - cell
    second_cell = lax.rem(second, 4)
    other = 1 - core
    far_rank = lax.rem(rank + ranks // 2, ranks)
    onward_rank = lax.rem(rank + 2 - 4 * side + ranks, ranks)
    behind_rank = lax.rem(rank - 2 + 4 * side + ranks, ranks)

    loads, sends = [], []

    def load(source, target):
        copy = pltpu.make_async_copy(source, target, load_sem.at[len(loads)])
        copy.start()
        loads.append(copy)
        return copy

    def send(source, target, to_core, to_rank):
        spot = len(sends)
        copy = pltpu.make_async_remote_copy(
            src_ref=source,
            dst_ref=target,
            send_sem=send_sem.at[spot],
            recv_sem=recv_sem.at[spot],
            device_id=(to_core, to_rank),
            device_id_type=MESH,
        )
        copy.start()
        sends.append(copy)
        return copy

    barrier = pltpu.get_barrier_semaphore()
    peers = [(other, rank), (core, across_side), (core, across_up)]
    peers += [(core, lax.rem(rank + 4 * step, ranks)) for step in range(1, line)]
    peers += [(core, onward_rank), (core, behind_rank), (core, far_rank)]
    for peer in peers:
        pl.semaphore_signal(barrier, inc=1, device_id=peer, device_id_type=MESH)

    attend_loads = {}
    for request in reversed(range(requests)):
        attend_loads[request] = (
            load(query_hbm.at[:, 0, request], query.at[request]),
            load(cache_hbm.at[0, request], cache.at[request]),
        )
    parts = 4
    rows = width // parts
    gate_loads = []
    for part in range(parts):
        span = pl.ds(part * rows, rows)
        gate_loads.append(
            (load(gate_hbm.at[0, span], w_gate.at[span]), load(up_hbm.at[0, span], w_up.at[span]))
        )
    down_load = load(down_hbm.at[0], w_down)

    lane = lax.broadcasted_iota(jnp.int32, (requests, LANES), 1)
    expert = lane - jnp.where(lane >= 2 * ranks, 2 * ranks, jnp.where(lane >= ranks, ranks, 0))
    dense = []
    for step in range(steps):
        logits = logits_ref[step, 0].astype(jnp.float32)
        chosen = routes_ref[step, 0]
        sigmoid_part = 1.0 / (1.0 + jnp.exp(-logits))
        gates = 2.5 * sigmoid_part / jnp.sum(sigmoid_part, 1, keepdims=True)
        total = jnp.zeros((requests, LANES), jnp.float32)
        for k in range(chosen.shape[1]):
            total = total + jnp.where(chosen[:, k : k + 1] == expert, gates[:, k : k + 1], 0.0)
        dense.append(total)
    dense = jnp.concatenate(dense, 0)
    lane = lax.broadcasted_iota(jnp.int32, (own_rows, LANES), 1)
    high = dense.astype(jnp.bfloat16).astype(jnp.float32)
    middle = (dense - high).astype(jnp.bfloat16).astype(jnp.float32)
    low = dense - high - middle
    coded = jnp.where(lane < ranks, high, jnp.where(lane < 2 * ranks, middle, low))
    coded = jnp.where(lane < 3 * ranks, coded, 0.0)
    own = jnp.concatenate(
        [hidden_ref[step, 0].astype(jnp.float32) for step in range(steps)], 0
    )
    for block in range(blocks):
        column[place, block] = own[:, block * LANES : (block + 1) * LANES].astype(jnp.bfloat16)
    column[place, blocks] = coded.astype(jnp.bfloat16)

    pl.semaphore_wait(barrier, len(peers))

    cuts = [blocks * c // GATHER_CHUNKS for c in range(GATHER_CHUNKS)] + [layers]
    spans = [pl.ds(cuts[c], cuts[c + 1] - cuts[c]) for c in range(GATHER_CHUNKS)]
    line_sends = []
    for span in spans:
        line_sends.append(
            [
                send(
                    column.at[place, span],
                    column.at[place, span],
                    core,
                    lax.rem(rank + 4 * step, ranks),
                )
                for step in range(1, line)
            ]
        )

    def attend(request):
        for copy in attend_loads[request]:
            copy.wait()
        length = lengths_ref[request, rank]
        scale = HEAD_QK ** (-0.5)
        lines = jnp.concatenate([query[request, step] for step in range(steps)], 1)
        keys = cache[request]
        scores = (
            lax.dot_general(
                lines, keys, (((0,), (0,)), ((), ())), preferred_element_type=jnp.float32
            )
            * scale
        )
        spot = lax.broadcasted_iota(jnp.int32, scores.shape, 1)
        scores = jnp.where(spot < length, scores, -jnp.inf)
        row_step = lax.broadcasted_iota(jnp.int32, (steps * heads, 1), 0) // heads
        fresh = [
            fresh_ref[step, 0].astype(jnp.float32)[request : request + 1] for step in range(steps)
        ]
        pad = jnp.zeros((16 - steps, lat), jnp.float32)
        fresh_keys = jnp.concatenate(fresh + [pad], 0).astype(jnp.bfloat16)
        fresh_all = (
            lax.dot_general(
                lines, fresh_keys, (((0,), (1,)), ((), ())), preferred_element_type=jnp.float32
            )
            * scale
        )
        row_max = jnp.max(scores, 1, keepdims=True)
        fresh_scores = []
        for step in range(steps):
            one = jnp.where(row_step >= step, fresh_all[:, step : step + 1], -jnp.inf)
            row_max = jnp.maximum(row_max, one)
            fresh_scores.append(one)
        weights = jnp.exp(scores - row_max)
        fresh_weights = [jnp.exp(one - row_max) for one in fresh_scores]
        total = jnp.sum(weights, 1, keepdims=True)
        for one in fresh_weights:
            total = total + one
        share = 1.0 / total
        probs = (weights * share).astype(jnp.bfloat16)
        result = lax.dot_general(
            probs, keys[:KV_RANK], (((1,), (1,)), ((), ())), preferred_element_type=jnp.float32
        )
        for step in range(steps):
            part = (fresh_weights[step] * share).astype(jnp.bfloat16).astype(jnp.float32)
            result = result + part * fresh[step][:, :KV_RANK]
        result = result.astype(jnp.bfloat16)
        for step in range(steps):
            served[request, step] = result[step * heads : (step + 1) * heads]

    attend(1)

    mine = core * half + cell
    first_sends, pair_sends = [], []
    for c, span in enumerate(spans):
        for copy in line_sends[c]:
            copy.wait_recv()
        merged = [column[spot, span].astype(jnp.float32) for spot in range(line)]
        tokens[mine, span] = jnp.concatenate(merged, 1).astype(jnp.bfloat16)
        first_sends.append(send(tokens.at[mine, span], tokens.at[mine, span], core, first))
        pair_sends.append([send(tokens.at[mine, span], tokens.at[mine, span], other, rank)])

    attend(0)

    second_sends = []
    near_block = core * half + first_cell
    for c, span in enumerate(spans):
        first_sends[c].wait_recv()
        second_sends.append(
            [
                send(tokens.at[block, span], tokens.at[block, span], core, second)
                for block in (mine, near_block)
            ]
        )
        pair_sends[c].append(
            send(tokens.at[near_block, span], tokens.at[near_block, span], other, rank)
        )
    far_send = send(served.at[0], far, core, far_rank)
    near_send = send(served.at[1], near, core, across_side)

    gate_part = jnp.zeros((2 * half * line * own_rows, w_gate.shape[1]), jnp.float32)
    up_part = gate_part
    piece = blocks // parts
    done = 0
    for c, span in enumerate(spans):
        for copy, block in zip(second_sends[c], (core * half + second_cell, core * half + corner)):
            copy.wait_recv()
            pair_sends[c].append(
                send(tokens.at[block, span], tokens.at[block, span], other, rank)
            )
        for copy in pair_sends[c]:
            copy.wait_recv()
        while done < parts and (done + 1) * piece <= cuts[c + 1]:
            for copy in gate_loads[done]:
                copy.wait()
            pieces = [
                tokens[:, block].reshape(gate_part.shape[0], LANES)
                for block in range(done * piece, (done + 1) * piece)
            ]
            values = jnp.concatenate(pieces, 1)
            span_rows = pl.ds(done * rows, rows)
            gate_part = gate_part + jnp.dot(
                values, w_gate[span_rows], preferred_element_type=jnp.float32
            )
            up_part = up_part + jnp.dot(
                values, w_up[span_rows], preferred_element_type=jnp.float32
            )
            done += 1
    units = (gate_part / (1.0 + jnp.exp(-gate_part)) * up_part).astype(jnp.bfloat16)
    coded = tokens[:, blocks].reshape(gate_part.shape[0], LANES).astype(jnp.float32)
    lane = lax.broadcasted_iota(jnp.int32, coded.shape, 1)
    hit = (lane == rank) | (lane == rank + ranks) | (lane == rank + 2 * ranks)
    gain = jnp.sum(jnp.where(hit, coded, 0.0), 1, keepdims=True)
    down_load.wait()

    chunk = width // RETURN_CHUNKS
    side_rows = half * line * own_rows
    cell_rows = line * own_rows
    pairs, firsts, seconds, lines = {}, {}, {}, {}

    def stage_down(c):
        out = jnp.dot(
            units, w_down[:, c * chunk : (c + 1) * chunk], preferred_element_type=jnp.float32
        )
        out = out * gain
        for part in range(2):
            value = out[part * side_rows : (part + 1) * side_rows]
            own_part[c, part] = value
            pair_send[c, part] = value.astype(jnp.bfloat16)
        pairs[c] = send(pair_send.at[c, other], pair_recv.at[c], other, rank)

    def stage_chip(c):
        pairs[c].wait_recv()
        value = own_part[c, core] + pair_recv[c].astype(jnp.float32)
        for part in range(half):
            cut = value[part * cell_rows : (part + 1) * cell_rows]
            chip_part[c, part] = cut
            chip_send[c, part] = cut.astype(jnp.bfloat16)
        firsts[c] = [
            send(chip_send.at[c, corner], first_recv.at[c, 1], core, second),
            send(chip_send.at[c, second_cell], first_recv.at[c, 0], core, second),
        ]

    def stage_plane(c):
        firsts[c][0].wait_recv()
        value = chip_part[c, first_cell] + first_recv[c, 1].astype(jnp.float32)
        second_send[c] = value.astype(jnp.bfloat16)
        seconds[c] = send(second_send.at[c], second_recv.at[c], core, first)
        firsts[c][1].wait_recv()
        second_keep[c] = chip_part[c, cell] + first_recv[c, 0].astype(jnp.float32)

    def stage_line(c):
        seconds[c].wait_recv()
        value = second_keep[c] + second_recv[c].astype(jnp.float32)
        for spot in range(line):
            cut = value[spot * own_rows : (spot + 1) * own_rows]
            line_part[c, spot] = cut
            line_send[c, spot] = cut.astype(jnp.bfloat16)
        lines[c] = [
            send(
                line_send.at[c, lax.rem(place + step, line)],
                line_recv.at[c, step - 1],
                core,
                lax.rem(rank + 4 * step, ranks),
            )
            for step in range(1, line)
        ]

    def stage_sum(c):
        value = line_part[c, place]
        for step in range(1, line):
            lines[c][step - 1].wait_recv()
            value = value + line_recv[c, step - 1].astype(jnp.float32)
        value = value.astype(jnp.bfloat16)
        for step in range(steps):
            moe_ref[step, 0, :, c * chunk : (c + 1) * chunk] = value[
                step * requests : (step + 1) * requests
            ]

    stages = (stage_down, stage_chip, stage_plane, stage_line, stage_sum)
    stores = []

    def settle(request, value):
        moved[request] = value
        stores.append(load(moved.at[request], attended_hbm.at[:, 0, request]))

    for turn in range(RETURN_CHUNKS + len(stages) - 1):
        for depth, stage in enumerate(stages):
            if 0 <= turn - depth < RETURN_CHUNKS:
                stage(turn - depth)
        if turn == 1:
            near_send.wait_recv()
            onward_send = send(near, onward, core, onward_rank)
        if turn == RETURN_CHUNKS + 2:
            far_send.wait_recv()
            settle(0, jnp.where(homes_ref[0, rank] == rank, served[0], far[...]))
    onward_send.wait_recv()
    home = homes_ref[1, rank]
    arrived = jnp.where(home == across_side, near[...], onward[...])
    settle(1, jnp.where(home == rank, served[1], arrived))
    for copy in sends:
        copy.wait_send()
    for copy in stores:
        copy.wait()


def ladder(
    latent_cache,
    lengths,
    new_home,
    queries,
    new_latent,
    hidden,
    routes,
    route_logits,
    w_gate,
    w_up,
    w_down,
):
    ranks, slices = lax.axis_size("ep"), lax.axis_size("dp")
    line = ranks // 4
    steps, _, requests, width = hidden.shape
    heads, lat = queries.shape[3:]
    keys = latent_cache.shape[2]
    units = w_gate.shape[2]
    layers = width // LANES + 1
    own_rows = steps * requests
    chunk = width // RETURN_CHUNKS
    cell_rows = line * own_rows
    bf16, f32 = jnp.bfloat16, jnp.float32
    vmem = pl.BlockSpec(memory_space=pltpu.VMEM)
    smem = pl.BlockSpec(memory_space=pltpu.SMEM)
    hbm = pl.BlockSpec(memory_space=pl.ANY)
    gather_sends = GATHER_CHUNKS * (line - 1 + 1 + 2 + 4)
    return_sends = RETURN_CHUNKS * (1 + 2 + 1 + line - 1)
    sends = gather_sends + return_sends + 3
    loads = 2 * requests + 8 + 1 + requests
    return pl.pallas_call(
        functools.partial(ladder_kernel, dict(ranks=ranks, line=line)),
        out_shape=(
            jax.ShapeDtypeStruct((steps, 1, requests, heads, KV_RANK), bf16),
            jax.ShapeDtypeStruct((steps, 1, requests, width), bf16),
        ),
        in_specs=[smem, smem, vmem, vmem, vmem, vmem] + [hbm] * 5,
        out_specs=(hbm, vmem),
        scratch_shapes=[
            pltpu.VMEM((line, layers, own_rows, LANES), bf16),
            pltpu.VMEM((slices * 4, layers, cell_rows, LANES), bf16),
            pltpu.VMEM((requests, steps, lat, heads), bf16),
            pltpu.VMEM((requests, lat, keys), bf16),
            pltpu.VMEM((width, units), bf16),
            pltpu.VMEM((width, units), bf16),
            pltpu.VMEM((units, width), bf16),
            pltpu.VMEM((requests, steps, heads, KV_RANK), bf16),
            pltpu.VMEM((steps, heads, KV_RANK), bf16),
            pltpu.VMEM((steps, heads, KV_RANK), bf16),
            pltpu.VMEM((steps, heads, KV_RANK), bf16),
            pltpu.VMEM((requests, steps, heads, KV_RANK), bf16),
            pltpu.VMEM((RETURN_CHUNKS, 2, 4 * cell_rows, chunk), f32),
            pltpu.VMEM((RETURN_CHUNKS, 2, 4 * cell_rows, chunk), bf16),
            pltpu.VMEM((RETURN_CHUNKS, 4 * cell_rows, chunk), bf16),
            pltpu.VMEM((RETURN_CHUNKS, 4, cell_rows, chunk), f32),
            pltpu.VMEM((RETURN_CHUNKS, 4, cell_rows, chunk), bf16),
            pltpu.VMEM((RETURN_CHUNKS, 2, cell_rows, chunk), bf16),
            pltpu.VMEM((RETURN_CHUNKS, cell_rows, chunk), f32),
            pltpu.VMEM((RETURN_CHUNKS, cell_rows, chunk), bf16),
            pltpu.VMEM((RETURN_CHUNKS, cell_rows, chunk), bf16),
            pltpu.VMEM((RETURN_CHUNKS, line, own_rows, chunk), f32),
            pltpu.VMEM((RETURN_CHUNKS, line, own_rows, chunk), bf16),
            pltpu.VMEM((RETURN_CHUNKS, line - 1, own_rows, chunk), bf16),
            pltpu.SemaphoreType.DMA((loads,)),
            pltpu.SemaphoreType.DMA((sends,)),
            pltpu.SemaphoreType.DMA((sends,)),
        ],
        compiler_params=pltpu.CompilerParams(
            collective_id=0, has_side_effects=True, vmem_limit_bytes=56 * 1024 * 1024
        ),
        name="ladder",
    )(
        lengths.T,
        new_home.T,
        new_latent,
        hidden,
        routes,
        route_logits,
        jnp.swapaxes(latent_cache, 2, 3),
        jnp.swapaxes(queries, 3, 4),
        w_gate,
        w_up,
        w_down,
    )


def attend_kernel(length_ref, query_ref, cache_ref, fresh_ref, out_ref):
    step_count, head_count, lat_width = query_ref.shape
    rows = step_count * head_count
    length = length_ref[pl.program_id(0)]
    scale = HEAD_QK ** (-0.5)
    query = query_ref[...].reshape(rows, lat_width)
    keys = cache_ref[...]
    scores = (
        lax.dot_general(
            query, keys, (((1,), (1,)), ((), ())), preferred_element_type=jnp.float32
        )
        * scale
    )
    place = lax.broadcasted_iota(jnp.int32, scores.shape, 1)
    scores = jnp.where(place < length, scores, -jnp.inf)
    row_step = lax.broadcasted_iota(jnp.int32, (rows, 1), 0) // head_count
    wide_query = query.astype(jnp.float32)
    fresh = fresh_ref[...].astype(jnp.float32)
    fresh_scores = []
    row_max = jnp.max(scores, 1, keepdims=True)
    for step in range(step_count):
        one = jnp.sum(wide_query * fresh[step : step + 1], 1, keepdims=True) * scale
        one = jnp.where(row_step >= step, one, -jnp.inf)
        row_max = jnp.maximum(row_max, one)
        fresh_scores.append(one)
    weights = jnp.exp(scores - row_max)
    fresh_weights = [jnp.exp(one - row_max) for one in fresh_scores]
    total = jnp.sum(weights, 1, keepdims=True)
    for one in fresh_weights:
        total = total + one
    probs = (weights / total).astype(jnp.bfloat16)
    served = jnp.dot(probs, keys[:, :KV_RANK], preferred_element_type=jnp.float32)
    for step in range(step_count):
        part = (fresh_weights[step] / total).astype(jnp.bfloat16).astype(jnp.float32)
        served = served + part * fresh[step : step + 1, :KV_RANK]
    out_ref[...] = served.astype(jnp.bfloat16).reshape(step_count, head_count, KV_RANK)


def attend(own_lengths, queries, cache, fresh):
    step_count, _, requests, heads, lat = queries.shape
    keys = cache.shape[2]
    return pl.pallas_call(
        attend_kernel,
        grid_spec=pltpu.PrefetchScalarGridSpec(
            num_scalar_prefetch=1,
            grid=(requests,),
            in_specs=[
                pl.BlockSpec((step_count, None, None, heads, lat), lambda r, n: (0, 0, r, 0, 0)),
                pl.BlockSpec((None, None, keys, lat), lambda r, n: (0, r, 0, 0)),
                pl.BlockSpec((None, step_count, lat), lambda r, n: (r, 0, 0)),
            ],
            out_specs=pl.BlockSpec((None, step_count, heads, KV_RANK), lambda r, n: (r, 0, 0, 0)),
        ),
        out_shape=jax.ShapeDtypeStruct((requests, step_count, heads, KV_RANK), jnp.bfloat16),
        name="attend",
    )(own_lengths, queries, cache, fresh)


def travel(even, odd, ranks):
    half = ranks // 2
    across = [(e, (e + half) % ranks) for e in range(ranks)]
    ahead = [(e, (e + 1) % ranks) for e in range(ranks)]
    behind = [(e, (e - 1) % ranks) for e in range(ranks)]
    far = lax.ppermute(even, "ep", across)
    left = lax.ppermute(odd, "ep", ahead)
    right = lax.ppermute(odd, "ep", behind)
    return far, left, right


def relocate(computed, arrived, new_home, ranks, own_rank):
    requests = computed.shape[0]
    far, left, right = arrived
    anchor = new_home[own_rank]
    results = []
    for request in range(requests):
        home, slot = anchor[request], request // 2
        if request % 2 == 0:
            moved = far[slot]
        else:
            moved = jnp.where(home == (own_rank + 1) % ranks, right[slot], left[slot])
        results.append(jnp.where(home == own_rank, computed[request], moved))
    return jnp.stack(results, 1)[:, None]


def shards(
    latent_cache,
    lengths,
    new_home,
    queries,
    new_latent,
    hidden,
    routes,
    route_logits,
    w_gate,
    w_up,
    w_down,
):
    ranks = lax.axis_size("ep")
    own_rank = lax.axis_index("ep")
    step_count, _, requests, width = hidden.shape
    own_rows = step_count * requests
    slices = lax.axis_size("dp")

    def shift(value, step):
        return lax.ppermute(value, "dp", [(i, (i + step) % slices) for i in range(slices)])

    rows = hidden.reshape(own_rows, width)
    copies = jnp.broadcast_to(rows[None], (ranks, own_rows, width))
    mine = lax.all_to_all(copies, "ep", split_axis=0, concat_axis=0, tiled=True)
    mine = mine.reshape(ranks * own_rows, width)

    computed = attend(
        lengths[own_rank], queries, latent_cache, jnp.swapaxes(new_latent[:, 0], 0, 1)
    )
    mine, computed, even, odd = lax.optimization_barrier(
        (mine, computed, computed[0::2], computed[1::2])
    )
    arrived = travel(even, odd, ranks)

    tokens = jnp.concatenate([mine] + [shift(mine, step) for step in range(1, slices)], 0)
    gate_part = jnp.dot(tokens, w_gate[0], preferred_element_type=jnp.float32)
    up_part = jnp.dot(tokens, w_up[0], preferred_element_type=jnp.float32)
    units = (jax.nn.silu(gate_part) * up_part).astype(jnp.bfloat16)
    slice_out = jnp.dot(units, w_down[0], preferred_element_type=jnp.float32)
    slice_out = slice_out.astype(jnp.bfloat16)
    parts = slice_out.reshape(slices, ranks * own_rows, width)
    whole = parts[0].astype(jnp.float32)
    for step in range(1, slices):
        whole = whole + shift(parts[step], -step).astype(jnp.float32)
    whole = whole.astype(jnp.bfloat16)
    whole, arrived = lax.optimization_barrier((whole, arrived))
    returned = lax.all_to_all(
        whole.reshape(ranks, own_rows, width), "ep", split_axis=0, concat_axis=0, tiled=True
    )

    attended = relocate(computed, arrived, new_home, ranks, own_rank)
    sigmoid_part = jax.nn.sigmoid(route_logits[:, 0].astype(jnp.float32))
    gates = 2.5 * sigmoid_part / jnp.sum(sigmoid_part, -1, keepdims=True)
    rank_ids = jnp.arange(ranks, dtype=jnp.int32)
    chosen = routes[:, 0, :, :, None] == rank_ids
    dense = jnp.sum(jnp.where(chosen, gates[..., None], 0.0), 2).reshape(own_rows, ranks)
    summed = jnp.sum(returned.astype(jnp.float32) * dense.T[:, :, None], 0)
    moe_out = summed.astype(jnp.bfloat16).reshape(step_count, 1, requests, width)
    return (attended, moe_out)


def solution(mesh):
    placed = (
        P("ep", "dp", None, None),
        P(None, "dp"),
        P(None, "dp"),
        P(None, "ep", "dp", None, None),
        P(None, "ep", "dp", None),
        P(None, "ep", "dp", None),
        P(None, "ep", "dp", None),
        P(None, "ep", "dp", None),
        P("ep", None, "dp"),
        P("ep", None, "dp"),
        P("ep", "dp", None),
    )
    out_specs = (P(None, "ep", "dp", None, None), P(None, "ep", "dp", None))
    ranks = mesh.shape["ep"]
    if mesh.shape["dp"] == 2 and ranks % 8 == 0 and 3 * ranks <= LANES:
        return jax.shard_map(
            ladder, mesh=mesh, in_specs=placed, out_specs=out_specs, check_vma=False
        )
    return jax.shard_map(
        shards,
        mesh=mesh,
        in_specs=placed,
        out_specs=out_specs,
        check_vma=False,
    )
```

profile of v0, /device:TPU:0, one launch (start us, length us, event | category | flops | bytes accessed | tf_op | source)
XLA Modules:
  0.0 49.3 jit_solution(1658959247097626609)
XLA Ops:
  0.6 45.4 %ladder.1 = (bf16[2,1,2,128,512]{4,3,2,1,0:T(8,128)(2,1)}, bf16[2,1,2,3584]{3,2,1,0:T(2,128)(2,1)}) custom-call(s32[2,16]{1,0:T(2,128)} %bitcast.6, s32[2,16]{1,0:T(2,128)} %bitcast.7, bf16[2,1,2,576]{3,2,1,0:T(2,128)(2,1)} %fresh_ref.1, bf16[2,1,2,3584]{3,2,1,0:T(2,128)(2,1)} %hidden_ref.1, s32[2,1,2,8]{3,2,1,0:T(2,128)} %routes_ref.1, ...), custom_call_target="tpu_custom_call" | custom-call | tf_op jit(solution)/shard_map/ladder/pallas_call | solution.py:411
  46.0 1.9 %copy.15 = bf16[2,1,2,128,512]{4,3,2,1,0:T(8,128)(2,1)} copy(bf16[2,1,2,128,512]{4,3,2,1,0:T(8,128)(2,1)} %get-tuple-element.4) | data formatting | bytes 1048576
  47.9 1.4 %copy.16 = bf16[2,1,2,3584]{3,2,1,0:T(2,128)(2,1)} copy(bf16[2,1,2,3584]{3,2,1,0:T(2,128)(2,1)} %get-tuple-element.5) | data formatting | bytes 57344
where the time goes:
time: 49.6 us; the launch traced here: 49.3 us
  Pallas kernels  45.4 us (92%)
  local copies, waits for them, and re-layouts  3.25 us (7%)
  between operations  0.64 us (1%)
    pallas_call x1, Pallas kernels, ladder(): pl.pallas_call(functools.partial(ladder_kernel, dict(ranks=ranks, line=li...  45.4 us
    unnamed x2, local copies, waits for them, and re-layouts  3.25 us

commit v1 on v0

--- a/solution.py
+++ b/solution.py
@@ -18,18 +18,25 @@
 
 def ladder_kernel(
     plan,
+    lengths_hbm,
+    homes_hbm,
+    fresh_hbm,
+    hidden_hbm,
+    routes_hbm,
+    logits_hbm,
+    cache_hbm,
+    query_hbm,
+    gate_hbm,
+    up_hbm,
+    down_hbm,
+    attended_hbm,
+    moe_hbm,
     lengths_ref,
     homes_ref,
     fresh_ref,
     hidden_ref,
     routes_ref,
     logits_ref,
-    cache_hbm,
-    query_hbm,
-    gate_hbm,
-    up_hbm,
-    down_hbm,
-    attended_hbm,
     moe_ref,
     column,
     tokens,
@@ -80,7 +87,6 @@
     other = 1 - core
     far_rank = lax.rem(rank + ranks // 2, ranks)
     onward_rank = lax.rem(rank + 2 - 4 * side + ranks, ranks)
-    behind_rank = lax.rem(rank - 2 + 4 * side + ranks, ranks)
 
     loads, sends = [], []
 
@@ -107,10 +113,19 @@
     barrier = pltpu.get_barrier_semaphore()
     peers = [(other, rank), (core, across_side), (core, across_up)]
     peers += [(core, lax.rem(rank + 4 * step, ranks)) for step in range(1, line)]
-    peers += [(core, onward_rank), (core, behind_rank), (core, far_rank)]
     for peer in peers:
         pl.semaphore_signal(barrier, inc=1, device_id=peer, device_id_type=MESH)
 
+    token_loads = [
+        load(hidden_hbm, hidden_ref),
+        load(routes_hbm, routes_ref),
+        load(logits_hbm, logits_ref),
+    ]
+    small_loads = [
+        load(fresh_hbm, fresh_ref),
+        load(lengths_hbm, lengths_ref),
+        load(homes_hbm, homes_ref),
+    ]
     attend_loads = {}
     for request in reversed(range(requests)):
         attend_loads[request] = (
@@ -127,6 +142,8 @@
         )
     down_load = load(down_hbm.at[0], w_down)
 
+    for copy in token_loads:
+        copy.wait()
     lane = lax.broadcasted_iota(jnp.int32, (requests, LANES), 1)
     expert = lane - jnp.where(lane >= 2 * ranks, 2 * ranks, jnp.where(lane >= ranks, ranks, 0))
     dense = []
@@ -221,7 +238,12 @@
         for step in range(steps):
             served[request, step] = result[step * heads : (step + 1) * heads]
 
+    for copy in small_loads:
+        copy.wait()
     attend(1)
+    near_sends = [send(served.at[1, 0], near.at[0], core, across_side)]
+    attend(0)
+    far_sends = [send(served.at[0, step], far.at[step], core, far_rank) for step in range(steps)]
 
     mine = core * half + cell
     first_sends, pair_sends = [], []
@@ -233,8 +255,6 @@
         first_sends.append(send(tokens.at[mine, span], tokens.at[mine, span], core, first))
         pair_sends.append([send(tokens.at[mine, span], tokens.at[mine, span], other, rank)])
 
-    attend(0)
-
     second_sends = []
     near_block = core * half + first_cell
     for c, span in enumerate(spans):
@@ -248,8 +268,6 @@
         pair_sends[c].append(
             send(tokens.at[near_block, span], tokens.at[near_block, span], other, rank)
         )
-    far_send = send(served.at[0], far, core, far_rank)
-    near_send = send(served.at[1], near, core, across_side)
 
     gate_part = jnp.zeros((2 * half * line * own_rows, w_gate.shape[1]), jnp.float32)
     up_part = gate_part
@@ -261,6 +279,13 @@
             pair_sends[c].append(
                 send(tokens.at[block, span], tokens.at[block, span], other, rank)
             )
+        if c == GATHER_CHUNKS - 1:
+            near_sends += [
+                send(served.at[1, step], near.at[step], core, across_side)
+                for step in range(1, steps)
+            ]
+            near_sends[0].wait_recv()
+            onward_sends = [send(near.at[0], onward.at[0], core, onward_rank)]
         for copy in pair_sends[c]:
             copy.wait_recv()
         while done < parts and (done + 1) * piece <= cuts[c + 1]:
@@ -350,27 +375,38 @@
                 step * requests : (step + 1) * requests
             ]
 
-    stages = (stage_down, stage_chip, stage_plane, stage_line, stage_sum)
     stores = []
 
-    def settle(request, value):
-        moved[request] = value
-        stores.append(load(moved.at[request], attended_hbm.at[:, 0, request]))
-
-    for turn in range(RETURN_CHUNKS + len(stages) - 1):
-        for depth, stage in enumerate(stages):
-            if 0 <= turn - depth < RETURN_CHUNKS:
-                stage(turn - depth)
-        if turn == 1:
-            near_send.wait_recv()
-            onward_send = send(near, onward, core, onward_rank)
-        if turn == RETURN_CHUNKS + 2:
-            far_send.wait_recv()
-            settle(0, jnp.where(homes_ref[0, rank] == rank, served[0], far[...]))
-    onward_send.wait_recv()
-    home = homes_ref[1, rank]
-    arrived = jnp.where(home == across_side, near[...], onward[...])
-    settle(1, jnp.where(home == rank, served[1], arrived))
+    def settle(request, step):
+        home = homes_ref[request, rank]
+        arrived = far[step]
+        if request % 2:
+            arrived = jnp.where(home == across_side, near[step], onward[step])
+        moved[request, step] = jnp.where(home == rank, served[request, step], arrived)
+        stores.append(load(moved.at[request, step], attended_hbm.at[step, 0, request]))
+
+    for c in range(RETURN_CHUNKS):
+        stage_down(c)
+    for c in range(RETURN_CHUNKS):
+        stage_chip(c)
+    for c in range(RETURN_CHUNKS):
+        stage_plane(c)
+    for step in range(1, steps):
+        near_sends[step].wait_recv()
+        onward_sends.append(send(near.at[step], onward.at[step], core, onward_rank))
+    for c in range(RETURN_CHUNKS):
+        stage_line(c)
+    for step in range(steps):
+        far_sends[step].wait_recv()
+        settle(0, step)
+    onward_sends[0].wait_recv()
+    settle(1, 0)
+    for c in range(RETURN_CHUNKS):
+        stage_sum(c)
+    stores.append(load(moe_ref, moe_hbm))
+    for step in range(1, steps):
+        onward_sends[step].wait_recv()
+        settle(1, step)
     for copy in sends:
         copy.wait_send()
     for copy in stores:
@@ -401,22 +437,27 @@
     chunk = width // RETURN_CHUNKS
     cell_rows = line * own_rows
     bf16, f32 = jnp.bfloat16, jnp.float32
-    vmem = pl.BlockSpec(memory_space=pltpu.VMEM)
-    smem = pl.BlockSpec(memory_space=pltpu.SMEM)
     hbm = pl.BlockSpec(memory_space=pl.ANY)
     gather_sends = GATHER_CHUNKS * (line - 1 + 1 + 2 + 4)
     return_sends = RETURN_CHUNKS * (1 + 2 + 1 + line - 1)
-    sends = gather_sends + return_sends + 3
-    loads = 2 * requests + 8 + 1 + requests
+    sends = gather_sends + return_sends + 3 * steps
+    loads = 6 + 2 * requests + 8 + 1 + requests * steps + 1
     return pl.pallas_call(
         functools.partial(ladder_kernel, dict(ranks=ranks, line=line)),
         out_shape=(
             jax.ShapeDtypeStruct((steps, 1, requests, heads, KV_RANK), bf16),
             jax.ShapeDtypeStruct((steps, 1, requests, width), bf16),
         ),
-        in_specs=[smem, smem, vmem, vmem, vmem, vmem] + [hbm] * 5,
-        out_specs=(hbm, vmem),
+        in_specs=[hbm] * 11,
+        out_specs=(hbm, hbm),
         scratch_shapes=[
+            pltpu.SMEM((requests, ranks), jnp.int32),
+            pltpu.SMEM((requests, ranks), jnp.int32),
+            pltpu.VMEM(new_latent.shape, bf16),
+            pltpu.VMEM(hidden.shape, bf16),
+            pltpu.VMEM(routes.shape, jnp.int32),
+            pltpu.VMEM(route_logits.shape, bf16),
+            pltpu.VMEM(hidden.shape, bf16),
             pltpu.VMEM((line, layers, own_rows, LANES), bf16),
             pltpu.VMEM((slices * 4, layers, cell_rows, LANES), bf16),
             pltpu.VMEM((requests, steps, lat, heads), bf16),

time: 49.6 us -> 40.7 us (0.82)
  Pallas kernels: 45.4 us -> 36.5 us
    pallas_call x1, Pallas kernels: 45.4 us -> 36.5 us  [ladder(): pl.pallas_call(functools.partial(ladder_kernel, dict(ranks=ranks, line=li...]
where the time goes in v1:
time: 40.7 us; the launch traced here: 40.4 us
  Pallas kernels  36.5 us (90%)
  local copies, waits for them, and re-layouts  3.25 us (8%)
  between operations  0.64 us (2%)
    pallas_call x1, Pallas kernels, ladder(): pl.pallas_call(functools.partial(ladder_kernel, dict(ranks=ranks, line=li...  36.5 us
    unnamed x2, local copies, waits for them, and re-layouts  3.25 us

profile of v1, /device:TPU:0, one launch (start us, length us, event | category | flops | bytes accessed | tf_op | source)
XLA Modules:
  0.0 40.4 jit_solution(13126363507867540570)
XLA Ops:
  0.6 36.5 %ladder.1 = (bf16[2,1,2,128,512]{4,3,2,1,0:T(8,128)(2,1)}, bf16[2,1,2,3584]{3,2,1,0:T(2,128)(2,1)}) custom-call(s32[2,16]{1,0:T(2,128)} %bitcast.6, s32[2,16]{1,0:T(2,128)} %bitcast.7, bf16[2,1,2,576]{3,2,1,0:T(2,128)(2,1)} %fresh_hbm.1, bf16[2,1,2,3584]{3,2,1,0:T(2,128)(2,1)} %hidden_hbm.1, s32[2,1,2,8]{3,2,1,0:T(2,128)} %routes_hbm.1, ...), custom_call_target="tpu_custom_call" | custom-call | tf_op jit(solution)/shard_map/ladder/pallas_call | solution.py:445
  37.2 1.9 %copy.15 = bf16[2,1,2,128,512]{4,3,2,1,0:T(8,128)(2,1)} copy(bf16[2,1,2,128,512]{4,3,2,1,0:T(8,128)(2,1)} %get-tuple-element.4) | data formatting | bytes 1048576
  39.0 1.4 %copy.16 = bf16[2,1,2,3584]{3,2,1,0:T(2,128)(2,1)} copy(bf16[2,1,2,3584]{3,2,1,0:T(2,128)(2,1)} %get-tuple-element.5) | data formatting | bytes 57344

commit v2 on v1

--- a/solution.py
+++ b/solution.py
@@ -29,15 +29,14 @@
     gate_hbm,
     up_hbm,
     down_hbm,
-    attended_hbm,
-    moe_hbm,
+    attended_ref,
+    moe_ref,
     lengths_ref,
     homes_ref,
     fresh_ref,
     hidden_ref,
     routes_ref,
     logits_ref,
-    moe_ref,
     column,
     tokens,
     query,
@@ -49,7 +48,7 @@
     far,
     near,
     onward,
-    moved,
+    beyond,
     own_part,
     pair_send,
     pair_recv,
@@ -80,13 +79,11 @@
     side, up, place = lax.rem(rank, 2), lax.rem(lax.div(rank, 2), 2), lax.div(rank, 4)
     cell = lax.rem(rank, 4)
     across_side, across_up = rank + 1 - 2 * side, rank + 2 - 4 * up
-    first = across_up * (1 - core) + across_side * core
-    second = across_side * (1 - core) + across_up * core
-    first_cell, corner = lax.rem(first, 4), 3 - cell
-    second_cell = lax.rem(second, 4)
+    diagonal = rank - cell + 3 - cell
+    plane = (diagonal, across_side, across_up)
     other = 1 - core
     far_rank = lax.rem(rank + ranks // 2, ranks)
-    onward_rank = lax.rem(rank + 2 - 4 * side + ranks, ranks)
+    beyond_rank = lax.rem(rank + 4 - 8 * side + ranks, ranks)
 
     loads, sends = [], []
 
@@ -111,7 +108,7 @@
         return copy
 
     barrier = pltpu.get_barrier_semaphore()
-    peers = [(other, rank), (core, across_side), (core, across_up)]
+    peers = [(other, rank)] + [(core, peer) for peer in plane]
     peers += [(core, lax.rem(rank + 4 * step, ranks)) for step in range(1, line)]
     for peer in peers:
         pl.semaphore_signal(barrier, inc=1, device_id=peer, device_id_type=MESH)
@@ -188,6 +185,23 @@
             ]
         )
 
+    near_sends, onward_sends, beyond_sends, far_sends = {}, {}, {}, {}
+    quarter = heads // 2
+
+    def cut(ref, piece):
+        return ref.at[piece // 2, pl.ds(piece % 2 * quarter, quarter)]
+
+    def send_near(piece):
+        near_sends[piece] = send(cut(served.at[1], piece), cut(near, piece), core, across_side)
+
+    def send_onward(piece):
+        near_sends[piece].wait_recv()
+        onward_sends[piece] = send(cut(near, piece), cut(onward, piece), core, across_up)
+
+    def send_beyond(piece):
+        onward_sends[piece].wait_recv()
+        beyond_sends[piece] = send(cut(onward, piece), cut(beyond, piece), core, beyond_rank)
+
     def attend(request):
         for copy in attend_loads[request]:
             copy.wait()
@@ -241,51 +255,38 @@
     for copy in small_loads:
         copy.wait()
     attend(1)
-    near_sends = [send(served.at[1, 0], near.at[0], core, across_side)]
+    send_near(0)
+    send_near(1)
     attend(0)
     far_sends = [send(served.at[0, step], far.at[step], core, far_rank) for step in range(steps)]
 
     mine = core * half + cell
-    first_sends, pair_sends = [], []
+    plane_sends, pair_sends = [], []
     for c, span in enumerate(spans):
         for copy in line_sends[c]:
             copy.wait_recv()
         merged = [column[spot, span].astype(jnp.float32) for spot in range(line)]
         tokens[mine, span] = jnp.concatenate(merged, 1).astype(jnp.bfloat16)
-        first_sends.append(send(tokens.at[mine, span], tokens.at[mine, span], core, first))
-        pair_sends.append([send(tokens.at[mine, span], tokens.at[mine, span], other, rank)])
-
-    second_sends = []
-    near_block = core * half + first_cell
-    for c, span in enumerate(spans):
-        first_sends[c].wait_recv()
-        second_sends.append(
-            [
-                send(tokens.at[block, span], tokens.at[block, span], core, second)
-                for block in (mine, near_block)
-            ]
-        )
-        pair_sends[c].append(
-            send(tokens.at[near_block, span], tokens.at[near_block, span], other, rank)
-        )
-
+        block = tokens.at[mine, span]
+        plane_sends.append([send(block, block, core, peer) for peer in plane])
+        pair_sends.append([send(block, block, other, rank)])
+
+    send_near(2)
+    send_near(3)
     gate_part = jnp.zeros((2 * half * line * own_rows, w_gate.shape[1]), jnp.float32)
     up_part = gate_part
     piece = blocks // parts
     done = 0
     for c, span in enumerate(spans):
-        for copy, block in zip(second_sends[c], (core * half + second_cell, core * half + corner)):
+        for copy, peer in zip(plane_sends[c], plane):
             copy.wait_recv()
+            block = core * half + lax.rem(peer, 4)
             pair_sends[c].append(
                 send(tokens.at[block, span], tokens.at[block, span], other, rank)
             )
         if c == GATHER_CHUNKS - 1:
-            near_sends += [
-                send(served.at[1, step], near.at[step], core, across_side)
-                for step in range(1, steps)
-            ]
-            near_sends[0].wait_recv()
-            onward_sends = [send(near.at[0], onward.at[0], core, onward_rank)]
+            send_onward(0)
+            send_onward(1)
         for copy in pair_sends[c]:
             copy.wait_recv()
         while done < parts and (done + 1) * piece <= cuts[c + 1]:
@@ -304,6 +305,8 @@
                 values, w_up[span_rows], preferred_element_type=jnp.float32
             )
             done += 1
+    send_onward(2)
+    send_onward(3)
     units = (gate_part / (1.0 + jnp.exp(-gate_part)) * up_part).astype(jnp.bfloat16)
     coded = tokens[:, blocks].reshape(gate_part.shape[0], LANES).astype(jnp.float32)
     lane = lax.broadcasted_iota(jnp.int32, coded.shape, 1)
@@ -327,7 +330,14 @@
             pair_send[c, part] = value.astype(jnp.bfloat16)
         pairs[c] = send(pair_send.at[c, other], pair_recv.at[c], other, rank)
 
+    def route():
+        turn = core
+        to_second = across_side * (1 - turn) + across_up * turn
+        to_first = across_up * (1 - turn) + across_side * turn
+        return to_first, to_second
+
     def stage_chip(c):
+        _, second = route()
         pairs[c].wait_recv()
         value = own_part[c, core] + pair_recv[c].astype(jnp.float32)
         for part in range(half):
@@ -335,13 +345,14 @@
             chip_part[c, part] = cut
             chip_send[c, part] = cut.astype(jnp.bfloat16)
         firsts[c] = [
-            send(chip_send.at[c, corner], first_recv.at[c, 1], core, second),
-            send(chip_send.at[c, second_cell], first_recv.at[c, 0], core, second),
+            send(chip_send.at[c, 3 - cell], first_recv.at[c, 1], core, second),
+            send(chip_send.at[c, lax.rem(second, 4)], first_recv.at[c, 0], core, second),
         ]
 
     def stage_plane(c):
+        first, _ = route()
         firsts[c][0].wait_recv()
-        value = chip_part[c, first_cell] + first_recv[c, 1].astype(jnp.float32)
+        value = chip_part[c, lax.rem(first, 4)] + first_recv[c, 1].astype(jnp.float32)
         second_send[c] = value.astype(jnp.bfloat16)
         seconds[c] = send(second_send.at[c], second_recv.at[c], core, first)
         firsts[c][1].wait_recv()
@@ -375,42 +386,40 @@
                 step * requests : (step + 1) * requests
             ]
 
-    stores = []
-
     def settle(request, step):
         home = homes_ref[request, rank]
         arrived = far[step]
         if request % 2:
-            arrived = jnp.where(home == across_side, near[step], onward[step])
-        moved[request, step] = jnp.where(home == rank, served[request, step], arrived)
-        stores.append(load(moved.at[request, step], attended_hbm.at[step, 0, request]))
+            arrived = jnp.where(side == up, beyond[step], onward[step])
+            arrived = jnp.where(home == across_side, near[step], arrived)
+        attended_ref[step, 0, request] = jnp.where(home == rank, served[request, step], arrived)
 
     for c in range(RETURN_CHUNKS):
         stage_down(c)
+    send_beyond(0)
+    send_beyond(1)
     for c in range(RETURN_CHUNKS):
         stage_chip(c)
+    send_beyond(2)
+    send_beyond(3)
     for c in range(RETURN_CHUNKS):
         stage_plane(c)
-    for step in range(1, steps):
-        near_sends[step].wait_recv()
-        onward_sends.append(send(near.at[step], onward.at[step], core, onward_rank))
     for c in range(RETURN_CHUNKS):
         stage_line(c)
     for step in range(steps):
         far_sends[step].wait_recv()
         settle(0, step)
-    onward_sends[0].wait_recv()
+    for piece in (0, 1):
+        beyond_sends[piece].wait_recv()
     settle(1, 0)
     for c in range(RETURN_CHUNKS):
         stage_sum(c)
-    stores.append(load(moe_ref, moe_hbm))
     for step in range(1, steps):
-        onward_sends[step].wait_recv()
+        for piece in (2, 3):
+            beyond_sends[piece].wait_recv()
         settle(1, step)
     for copy in sends:
         copy.wait_send()
-    for copy in stores:
-        copy.wait()
 
 
 def ladder(
@@ -438,18 +447,18 @@
     cell_rows = line * own_rows
     bf16, f32 = jnp.bfloat16, jnp.float32
     hbm = pl.BlockSpec(memory_space=pl.ANY)
-    gather_sends = GATHER_CHUNKS * (line - 1 + 1 + 2 + 4)
+    gather_sends = GATHER_CHUNKS * (line - 1 + 3 + 4)
     return_sends = RETURN_CHUNKS * (1 + 2 + 1 + line - 1)
-    sends = gather_sends + return_sends + 3 * steps
-    loads = 6 + 2 * requests + 8 + 1 + requests * steps + 1
+    sends = gather_sends + return_sends + 12 + steps
+    loads = 6 + 2 * requests + 8 + 1
     return pl.pallas_call(
         functools.partial(ladder_kernel, dict(ranks=ranks, line=line)),
         out_shape=(
-            jax.ShapeDtypeStruct((steps, 1, requests, heads, KV_RANK), bf16),
-            jax.ShapeDtypeStruct((steps, 1, requests, width), bf16),
+            pltpu.VMEM((steps, 1, requests, heads, KV_RANK), bf16),
+            pltpu.VMEM((steps, 1, requests, width), bf16),
         ),
         in_specs=[hbm] * 11,
-        out_specs=(hbm, hbm),
+        out_specs=(pl.BlockSpec(memory_space=pltpu.VMEM),) * 2,
         scratch_shapes=[
             pltpu.SMEM((requests, ranks), jnp.int32),
             pltpu.SMEM((requests, ranks), jnp.int32),
@@ -457,7 +466,6 @@
             pltpu.VMEM(hidden.shape, bf16),
             pltpu.VMEM(routes.shape, jnp.int32),
             pltpu.VMEM(route_logits.shape, bf16),
-            pltpu.VMEM(hidden.shape, bf16),
             pltpu.VMEM((line, layers, own_rows, LANES), bf16),
             pltpu.VMEM((slices * 4, layers, cell_rows, LANES), bf16),
             pltpu.VMEM((requests, steps, lat, heads), bf16),
@@ -469,7 +477,7 @@
             pltpu.VMEM((steps, heads, KV_RANK), bf16),
             pltpu.VMEM((steps, heads, KV_RANK), bf16),
             pltpu.VMEM((steps, heads, KV_RANK), bf16),
-            pltpu.VMEM((requests, steps, heads, KV_RANK), bf16),
+            pltpu.VMEM((steps, heads, KV_RANK), bf16),
             pltpu.VMEM((RETURN_CHUNKS, 2, 4 * cell_rows, chunk), f32),
             pltpu.VMEM((RETURN_CHUNKS, 2, 4 * cell_rows, chunk), bf16),
             pltpu.VMEM((RETURN_CHUNKS, 4 * cell_rows, chunk), bf16),

time: 40.7 us -> 36.6 us (0.90)
  Pallas kernels: 36.5 us -> 34.4 us
  local copies, waits for them, and re-layouts: 3.25 us -> 1.4 us
    pallas_call x1, Pallas kernels: 36.5 us -> 34.4 us  [ladder(): pl.pallas_call(functools.partial(ladder_kernel, dict(ranks=ranks, line=li...]
    unnamed x2, local copies, waits for them, and re-layouts: 3.25 us -> 1.4 us
where the time goes in v2:
time: 36.6 us; the launch traced here: 36.4 us
  Pallas kernels  34.4 us (94%)
  local copies, waits for them, and re-layouts  1.4 us (4%)
  between operations  0.64 us (2%)
    pallas_call x1, Pallas kernels, ladder(): pl.pallas_call(functools.partial(ladder_kernel, dict(ranks=ranks, line=li...  34.4 us
    unnamed x2, local copies, waits for them, and re-layouts  1.4 us

profile of v2, /device:TPU:0, one launch (start us, length us, event | category | flops | bytes accessed | tf_op | source)
XLA Modules:
  0.0 36.4 jit_solution(799903073899166884)
XLA Ops:
  0.6 34.4 %ladder.1 = (bf16[2,1,2,128,512]{4,3,2,1,0:T(8,128)(2,1)S(1)}, bf16[2,1,2,3584]{3,2,1,0:T(2,128)(2,1)S(1)}) custom-call(s32[2,16]{1,0:T(2,128)} %bitcast.6, s32[2,16]{1,0:T(2,128)} %bitcast.7, bf16[2,1,2,576]{3,2,1,0:T(2,128)(2,1)} %fresh_hbm.1, bf16[2,1,2,3584]{3,2,1,0:T(2,128)(2,1)} %hidden_hbm.1, s32[2,1,2,8]{3,2,1,0:T(2,128)} %routes_hbm.1, ...), custom_call_target="tpu_custom_call" | custom-call | tf_op jit(solution)/shard_map/ladder/pallas_call | solution.py:454
  35.0 0.8 %copy.15 = bf16[2,1,2,128,512]{4,3,2,1,0:T(8,128)(2,1)} copy(bf16[2,1,2,128,512]{4,3,2,1,0:T(8,128)(2,1)S(1)} %get-tuple-element.2) | data formatting | bytes 1048576
  35.8 0.6 %copy.16 = bf16[2,1,2,3584]{3,2,1,0:T(2,128)(2,1)} copy(bf16[2,1,2,3584]{3,2,1,0:T(2,128)(2,1)S(1)} %get-tuple-element.3) | data formatting | bytes 57344

commit v3 on v2

--- a/solution.py
+++ b/solution.py
@@ -12,7 +12,7 @@
 HEAD_QK = 192
 LANES = 128
 MESH = pl.DeviceIdType.MESH
-GATHER_CHUNKS = 2
+GATHER_CHUNKS = 1
 RETURN_CHUNKS = 4
 
 
@@ -181,7 +181,7 @@
                     core,
                     lax.rem(rank + 4 * step, ranks),
                 )
-                for step in range(1, line)
+                for step in reversed(range(1, line))
             ]
         )
 
@@ -330,14 +330,14 @@
             pair_send[c, part] = value.astype(jnp.bfloat16)
         pairs[c] = send(pair_send.at[c, other], pair_recv.at[c], other, rank)
 
-    def route():
-        turn = core
+    def route(c):
+        turn = core if c % 2 == 0 else other
         to_second = across_side * (1 - turn) + across_up * turn
         to_first = across_up * (1 - turn) + across_side * turn
         return to_first, to_second
 
     def stage_chip(c):
-        _, second = route()
+        _, second = route(c)
         pairs[c].wait_recv()
         value = own_part[c, core] + pair_recv[c].astype(jnp.float32)
         for part in range(half):
@@ -350,7 +350,7 @@
         ]
 
     def stage_plane(c):
-        first, _ = route()
+        first, _ = route(c)
         firsts[c][0].wait_recv()
         value = chip_part[c, lax.rem(first, 4)] + first_recv[c, 1].astype(jnp.float32)
         second_send[c] = value.astype(jnp.bfloat16)
@@ -420,6 +420,17 @@
         settle(1, step)
     for copy in sends:
         copy.wait_send()
+
+
+def settle_kernel(attended_ref, moe_ref, attended_hbm, moe_hbm, sems):
+    copies = (
+        pltpu.make_async_copy(attended_ref, attended_hbm, sems.at[0]),
+        pltpu.make_async_copy(moe_ref, moe_hbm, sems.at[1]),
+    )
+    for copy in copies:
+        copy.start()
+    for copy in copies:
+        copy.wait()
 
 
 def ladder(
@@ -451,7 +462,7 @@
     return_sends = RETURN_CHUNKS * (1 + 2 + 1 + line - 1)
     sends = gather_sends + return_sends + 12 + steps
     loads = 6 + 2 * requests + 8 + 1
-    return pl.pallas_call(
+    attended, moe_out = pl.pallas_call(
         functools.partial(ladder_kernel, dict(ranks=ranks, line=line)),
         out_shape=(
             pltpu.VMEM((steps, 1, requests, heads, KV_RANK), bf16),
@@ -511,6 +522,16 @@
         w_up,
         w_down,
     )
+    results = (attended, moe_out)
+    return pl.pallas_call(
+        settle_kernel,
+        out_shape=tuple(jax.ShapeDtypeStruct(one.shape, one.dtype) for one in results),
+        in_specs=[pl.BlockSpec(memory_space=pltpu.VMEM)] * 2,
+        out_specs=(hbm, hbm),
+        scratch_shapes=[pltpu.SemaphoreType.DMA((2,))],
+        compiler_params=pltpu.CompilerParams(vmem_limit_bytes=1024 * 1024),
+        name="settle",
+    )(*results)
 
 
 def attend_kernel(length_ref, query_ref, cache_ref, fresh_ref, out_ref):

time: 36.6 us -> 35.4 us (0.967)
  local copies, waits for them, and re-layouts: 1.4 us -> 0 us
    unnamed x2 -> x0, local copies, waits for them, and re-layouts: 1.4 us -> none
    pallas_call x0 -> x1, Pallas kernels: none -> 0.81 us  [ladder(): pl.pallas_call(settle_kernel, out_shape=tuple((jax.ShapeDtypeStruct(one.s...]
    pallas_call x1, Pallas kernels: 34.4 us -> 33.8 us  [ladder(): pl.pallas_call(functools.partial(ladder_kernel, dict(ranks=ranks, line=li...]
where the time goes in v3:
time: 35.4 us; the launch traced here: 35.3 us
  Pallas kernels  34.6 us (98%)
  between operations  0.64 us (2%)
    pallas_call x1, Pallas kernels, ladder(): pl.pallas_call(functools.partial(ladder_kernel, dict(ranks=ranks, line=li...  33.8 us
    pallas_call x1, Pallas kernels, ladder(): pl.pallas_call(settle_kernel, out_shape=tuple((jax.ShapeDtypeStruct(one.s...  0.81 us

profile of v3, /device:TPU:0, one launch (start us, length us, event | category | flops | bytes accessed | tf_op | source)
XLA Modules:
  0.0 35.3 jit_solution(13135518399820285254)
XLA Ops:
  0.6 33.8 %ladder.1 = (bf16[2,1,2,128,512]{4,3,2,1,0:T(8,128)(2,1)S(1)}, bf16[2,1,2,3584]{3,2,1,0:T(2,128)(2,1)S(1)}) custom-call(s32[2,16]{1,0:T(2,128)} %bitcast.6, s32[2,16]{1,0:T(2,128)} %bitcast.7, bf16[2,1,2,576]{3,2,1,0:T(2,128)(2,1)} %fresh_hbm.1, bf16[2,1,2,3584]{3,2,1,0:T(2,128)(2,1)} %hidden_hbm.1, s32[2,1,2,8]{3,2,1,0:T(2,128)} %routes_hbm.1, ...), custom_call_target="tpu_custom_call" | custom-call | tf_op jit(solution)/shard_map/ladder/pallas_call | solution.py:465
  34.4 0.8 %settle.1 = (bf16[2,1,2,128,512]{4,3,2,1,0:T(8,128)(2,1)}, bf16[2,1,2,3584]{3,2,1,0:T(2,128)(2,1)}) custom-call(bf16[2,1,2,128,512]{4,3,2,1,0:T(8,128)(2,1)S(1)} %get-tuple-element.4.attended_ref, bf16[2,1,2,3584]{3,2,1,0:T(2,128)(2,1)S(1)} %get-tuple-element.5.moe_ref), custom_call_target="tpu_custom_call" | custom-call | tf_op jit(solution)/shard_map/settle/pallas_call | solution.py:526

commit v4 on v3

--- a/solution.py
+++ b/solution.py
@@ -12,7 +12,6 @@
 HEAD_QK = 192
 LANES = 128
 MESH = pl.DeviceIdType.MESH
-GATHER_CHUNKS = 1
 RETURN_CHUNKS = 4
 
 
@@ -37,7 +36,7 @@
     hidden_ref,
     routes_ref,
     logits_ref,
-    column,
+    slots,
     tokens,
     query,
     cache,
@@ -61,6 +60,7 @@
     line_part,
     line_send,
     line_recv,
+    line_sems,
     load_sem,
     send_sem,
     recv_sem,
@@ -72,7 +72,6 @@
     heads = query.shape[-1]
     width = hidden_ref.shape[-1]
     blocks = width // LANES
-    layers = blocks + 1
     half = 4
     core = lax.axis_index("dp")
     rank = lax.axis_index("ep")
@@ -82,6 +81,7 @@
     diagonal = rank - cell + 3 - cell
     plane = (diagonal, across_side, across_up)
     other = 1 - core
+    mine = core * half + cell
     far_rank = lax.rem(rank + ranks // 2, ranks)
     beyond_rank = lax.rem(rank + 4 - 8 * side + ranks, ranks)
 
@@ -164,26 +164,35 @@
         [hidden_ref[step, 0].astype(jnp.float32) for step in range(steps)], 0
     )
     for block in range(blocks):
-        column[place, block] = own[:, block * LANES : (block + 1) * LANES].astype(jnp.bfloat16)
-    column[place, blocks] = coded.astype(jnp.bfloat16)
+        slots[mine, place, block] = own[:, block * LANES : (block + 1) * LANES].astype(jnp.bfloat16)
+    slots[mine, place, blocks] = coded.astype(jnp.bfloat16)
 
     pl.semaphore_wait(barrier, len(peers))
 
-    cuts = [blocks * c // GATHER_CHUNKS for c in range(GATHER_CHUNKS)] + [layers]
-    spans = [pl.ds(cuts[c], cuts[c + 1] - cuts[c]) for c in range(GATHER_CHUNKS)]
-    line_sends = []
-    for span in spans:
-        line_sends.append(
-            [
-                send(
-                    column.at[place, span],
-                    column.at[place, span],
-                    core,
-                    lax.rem(rank + 4 * step, ranks),
-                )
-                for step in reversed(range(1, line))
-            ]
-        )
+    def share(block, slot, to_core, to_rank):
+        return send(slots.at[block, slot], slots.at[block, slot], to_core, to_rank)
+
+    def spread(slot):
+        plane_sends.append([share(mine, slot, core, peer) for peer in plane])
+        pair_sends.append([share(mine, slot, other, rank)])
+
+    def arrival(step, slot):
+        return pltpu.make_async_remote_copy(
+            src_ref=slots.at[mine, slot],
+            dst_ref=slots.at[mine, slot],
+            send_sem=line_sems.at[0, step - 1],
+            recv_sem=line_sems.at[1, step - 1],
+            device_id=(core, lax.rem(rank + 4 * step, ranks)),
+            device_id_type=MESH,
+        )
+
+    def merge(block):
+        tokens[block] = jnp.concatenate([slots[block, slot] for slot in range(line)], 1)
+
+    plane_sends, pair_sends = [], []
+    for step in reversed(range(1, line)):
+        arrival(step, place).start()
+    spread(place)
 
     near_sends, onward_sends, beyond_sends, far_sends = {}, {}, {}, {}
     quarter = heads // 2
@@ -256,55 +265,51 @@
         copy.wait()
     attend(1)
     send_near(0)
-    send_near(1)
     attend(0)
     far_sends = [send(served.at[0, step], far.at[step], core, far_rank) for step in range(steps)]
 
-    mine = core * half + cell
-    plane_sends, pair_sends = [], []
-    for c, span in enumerate(spans):
-        for copy in line_sends[c]:
-            copy.wait_recv()
-        merged = [column[spot, span].astype(jnp.float32) for spot in range(line)]
-        tokens[mine, span] = jnp.concatenate(merged, 1).astype(jnp.bfloat16)
-        block = tokens.at[mine, span]
-        plane_sends.append([send(block, block, core, peer) for peer in plane])
-        pair_sends.append([send(block, block, other, rank)])
-
+    lower = place < line // 2
+    for reach in range(1, line):
+        step = jnp.where(lower, line - reach, reach)
+        slot = lax.rem(place - step + line, line)
+        arrival(step, slot).wait_recv()
+        spread(slot)
+    merge(mine)
+    send_near(1)
     send_near(2)
     send_near(3)
+    for reach in range(line):
+        slot = jnp.where(lower, place + reach, place - reach + line)
+        slot = lax.rem(slot, line)
+        for copy, peer in zip(plane_sends[reach], plane):
+            copy.wait_recv()
+            pair_sends[reach].append(share(core * half + lax.rem(peer, 4), slot, other, rank))
+    send_onward(0)
+    send_onward(1)
+    for peer in plane:
+        merge(core * half + lax.rem(peer, 4))
+    for copies in pair_sends:
+        for copy in copies:
+            copy.wait_recv()
+    for block in range(half):
+        merge(other * half + block)
+
     gate_part = jnp.zeros((2 * half * line * own_rows, w_gate.shape[1]), jnp.float32)
     up_part = gate_part
     piece = blocks // parts
-    done = 0
-    for c, span in enumerate(spans):
-        for copy, peer in zip(plane_sends[c], plane):
-            copy.wait_recv()
-            block = core * half + lax.rem(peer, 4)
-            pair_sends[c].append(
-                send(tokens.at[block, span], tokens.at[block, span], other, rank)
-            )
-        if c == GATHER_CHUNKS - 1:
-            send_onward(0)
-            send_onward(1)
-        for copy in pair_sends[c]:
-            copy.wait_recv()
-        while done < parts and (done + 1) * piece <= cuts[c + 1]:
-            for copy in gate_loads[done]:
-                copy.wait()
-            pieces = [
-                tokens[:, block].reshape(gate_part.shape[0], LANES)
-                for block in range(done * piece, (done + 1) * piece)
-            ]
-            values = jnp.concatenate(pieces, 1)
-            span_rows = pl.ds(done * rows, rows)
-            gate_part = gate_part + jnp.dot(
-                values, w_gate[span_rows], preferred_element_type=jnp.float32
-            )
-            up_part = up_part + jnp.dot(
-                values, w_up[span_rows], preferred_element_type=jnp.float32
-            )
-            done += 1
+    for done in range(parts):
+        for copy in gate_loads[done]:
+            copy.wait()
+        pieces = [
+            tokens[:, block].reshape(gate_part.shape[0], LANES)
+            for block in range(done * piece, (done + 1) * piece)
+        ]
+        values = jnp.concatenate(pieces, 1)
+        span_rows = pl.ds(done * rows, rows)
+        gate_part = gate_part + jnp.dot(
+            values, w_gate[span_rows], preferred_element_type=jnp.float32
+        )
+        up_part = up_part + jnp.dot(values, w_up[span_rows], preferred_element_type=jnp.float32)
     send_onward(2)
     send_onward(3)
     units = (gate_part / (1.0 + jnp.exp(-gate_part)) * up_part).astype(jnp.bfloat16)
@@ -420,6 +425,8 @@
         settle(1, step)
     for copy in sends:
         copy.wait_send()
+    for step in range(1, line):
+        arrival(step, place).wait_send()
 
 
 def settle_kernel(attended_ref, moe_ref, attended_hbm, moe_hbm, sems):
@@ -458,7 +465,7 @@
     cell_rows = line * own_rows
     bf16, f32 = jnp.bfloat16, jnp.float32
     hbm = pl.BlockSpec(memory_space=pl.ANY)
-    gather_sends = GATHER_CHUNKS * (line - 1 + 3 + 4)
+    gather_sends = line * (3 + 4)
     return_sends = RETURN_CHUNKS * (1 + 2 + 1 + line - 1)
     sends = gather_sends + return_sends + 12 + steps
     loads = 6 + 2 * requests + 8 + 1
@@ -477,7 +484,7 @@
             pltpu.VMEM(hidden.shape, bf16),
             pltpu.VMEM(routes.shape, jnp.int32),
             pltpu.VMEM(route_logits.shape, bf16),
-            pltpu.VMEM((line, layers, own_rows, LANES), bf16),
+            pltpu.VMEM((slices * 4, line, layers, own_rows, LANES), bf16),
             pltpu.VMEM((slices * 4, layers, cell_rows, LANES), bf16),
             pltpu.VMEM((requests, steps, lat, heads), bf16),
             pltpu.VMEM((requests, lat, keys), bf16),
@@ -501,6 +508,7 @@
             pltpu.VMEM((RETURN_CHUNKS, line, own_rows, chunk), f32),
             pltpu.VMEM((RETURN_CHUNKS, line, own_rows, chunk), bf16),
             pltpu.VMEM((RETURN_CHUNKS, line - 1, own_rows, chunk), bf16),
+            pltpu.SemaphoreType.DMA((2, line - 1)),
             pltpu.SemaphoreType.DMA((loads,)),
             pltpu.SemaphoreType.DMA((sends,)),
             pltpu.SemaphoreType.DMA((sends,)),

time: 35.4 us -> 34.3 us (0.969)
  Pallas kernels: 34.6 us -> 33.5 us
    pallas_call x1, Pallas kernels: 33.8 us -> 32.7 us  [ladder(): pl.pallas_call(functools.partial(ladder_kernel, dict(ranks=ranks, line=li...]
where the time goes in v4:
time: 34.3 us; the launch traced here: 34.2 us
  Pallas kernels  33.5 us (98%)
  between operations  0.64 us (2%)
    pallas_call x1, Pallas kernels, ladder(): pl.pallas_call(functools.partial(ladder_kernel, dict(ranks=ranks, line=li...  32.7 us
    pallas_call x1, Pallas kernels, ladder(): pl.pallas_call(settle_kernel, out_shape=tuple((jax.ShapeDtypeStruct(one.s...  0.81 us

profile of v4, /device:TPU:0, one launch (start us, length us, event | category | flops | bytes accessed | tf_op | source)
XLA Modules:
  0.0 34.2 jit_solution(3802148109516121016)
XLA Ops:
  0.6 32.7 %ladder.1 = (bf16[2,1,2,128,512]{4,3,2,1,0:T(8,128)(2,1)S(1)}, bf16[2,1,2,3584]{3,2,1,0:T(2,128)(2,1)S(1)}) custom-call(s32[2,16]{1,0:T(2,128)} %bitcast.6, s32[2,16]{1,0:T(2,128)} %bitcast.7, bf16[2,1,2,576]{3,2,1,0:T(2,128)(2,1)} %fresh_hbm.1, bf16[2,1,2,3584]{3,2,1,0:T(2,128)(2,1)} %hidden_hbm.1, s32[2,1,2,8]{3,2,1,0:T(2,128)} %routes_hbm.1, ...), custom_call_target="tpu_custom_call" | custom-call | tf_op jit(solution)/shard_map/ladder/pallas_call | solution.py:472
  33.4 0.8 %settle.1 = (bf16[2,1,2,128,512]{4,3,2,1,0:T(8,128)(2,1)}, bf16[2,1,2,3584]{3,2,1,0:T(2,128)(2,1)}) custom-call(bf16[2,1,2,128,512]{4,3,2,1,0:T(8,128)(2,1)S(1)} %get-tuple-element.4.attended_ref, bf16[2,1,2,3584]{3,2,1,0:T(2,128)(2,1)S(1)} %get-tuple-element.5.moe_ref), custom_call_target="tpu_custom_call" | custom-call | tf_op jit(solution)/shard_map/settle/pallas_call | solution.py:534

commit v5 on v4

--- a/solution.py
+++ b/solution.py
@@ -335,14 +335,10 @@
             pair_send[c, part] = value.astype(jnp.bfloat16)
         pairs[c] = send(pair_send.at[c, other], pair_recv.at[c], other, rank)
 
-    def route(c):
-        turn = core if c % 2 == 0 else other
-        to_second = across_side * (1 - turn) + across_up * turn
-        to_first = across_up * (1 - turn) + across_side * turn
-        return to_first, to_second
+    second = across_side * other + across_up * core
+    first = across_up * other + across_side * core
 
     def stage_chip(c):
-        _, second = route(c)
         pairs[c].wait_recv()
         value = own_part[c, core] + pair_recv[c].astype(jnp.float32)
         for part in range(half):
@@ -355,7 +351,6 @@
         ]
 
     def stage_plane(c):
-        first, _ = route(c)
         firsts[c][0].wait_recv()
         value = chip_part[c, lax.rem(first, 4)] + first_recv[c, 1].astype(jnp.float32)
         second_send[c] = value.astype(jnp.bfloat16)

time: 34.3 us -> 34 us (level)
  no operation moved by 1% of the time
where the time goes in v5:
time: 34 us; the launch traced here: 33.9 us
  Pallas kernels  33.2 us (98%)
  between operations  0.64 us (2%)
    pallas_call x1, Pallas kernels, ladder(): pl.pallas_call(functools.partial(ladder_kernel, dict(ranks=ranks, line=li...  32.4 us
    pallas_call x1, Pallas kernels, ladder(): pl.pallas_call(settle_kernel, out_shape=tuple((jax.ShapeDtypeStruct(one.s...  0.81 us

profile of v5, /device:TPU:0, one launch (start us, length us, event | category | flops | bytes accessed | tf_op | source)
XLA Modules:
  0.0 33.9 jit_solution(10685991490313433436)
XLA Ops:
  0.6 32.4 %ladder.1 = (bf16[2,1,2,128,512]{4,3,2,1,0:T(8,128)(2,1)S(1)}, bf16[2,1,2,3584]{3,2,1,0:T(2,128)(2,1)S(1)}) custom-call(s32[2,16]{1,0:T(2,128)} %bitcast.6, s32[2,16]{1,0:T(2,128)} %bitcast.7, bf16[2,1,2,576]{3,2,1,0:T(2,128)(2,1)} %fresh_hbm.1, bf16[2,1,2,3584]{3,2,1,0:T(2,128)(2,1)} %hidden_hbm.1, s32[2,1,2,8]{3,2,1,0:T(2,128)} %routes_hbm.1, ...), custom_call_target="tpu_custom_call" | custom-call | tf_op jit(solution)/shard_map/ladder/pallas_call | solution.py:467
  33.0 0.8 %settle.1 = (bf16[2,1,2,128,512]{4,3,2,1,0:T(8,128)(2,1)}, bf16[2,1,2,3584]{3,2,1,0:T(2,128)(2,1)}) custom-call(bf16[2,1,2,128,512]{4,3,2,1,0:T(8,128)(2,1)S(1)} %get-tuple-element.4.attended_ref, bf16[2,1,2,3584]{3,2,1,0:T(2,128)(2,1)S(1)} %get-tuple-element.5.moe_ref), custom_call_target="tpu_custom_call" | custom-call | tf_op jit(solution)/shard_map/settle/pallas_call | solution.py:529

commit v6 on v5

--- a/solution.py
+++ b/solution.py
@@ -12,7 +12,7 @@
 HEAD_QK = 192
 LANES = 128
 MESH = pl.DeviceIdType.MESH
-RETURN_CHUNKS = 4
+RETURN_CHUNKS = 2
 
 
 def ladder_kernel(
@@ -129,7 +129,7 @@
             load(query_hbm.at[:, 0, request], query.at[request]),
             load(cache_hbm.at[0, request], cache.at[request]),
         )
-    parts = 4
+    parts = 2
     rows = width // parts
     gate_loads = []
     for part in range(parts):
@@ -463,7 +463,7 @@
     gather_sends = line * (3 + 4)
     return_sends = RETURN_CHUNKS * (1 + 2 + 1 + line - 1)
     sends = gather_sends + return_sends + 12 + steps
-    loads = 6 + 2 * requests + 8 + 1
+    loads = 6 + 2 * requests + 4 + 1
     attended, moe_out = pl.pallas_call(
         functools.partial(ladder_kernel, dict(ranks=ranks, line=line)),
         out_shape=(

time: 34 us -> 34 us (level)
  no operation moved by 1% of the time
where the time goes in v6:
time: 34 us; the launch traced here: 33.9 us
  Pallas kernels  33.2 us (98%)
  between operations  0.64 us (2%)
    pallas_call x1, Pallas kernels, ladder(): pl.pallas_call(functools.partial(ladder_kernel, dict(ranks=ranks, line=li...  32.4 us
    pallas_call x1, Pallas kernels, ladder(): pl.pallas_call(settle_kernel, out_shape=tuple((jax.ShapeDtypeStruct(one.s...  0.81 us

profile of v6, /device:TPU:0, one launch (start us, length us, event | category | flops | bytes accessed | tf_op | source)
XLA Modules:
  0.0 33.9 jit_solution(11295920076379754489)
XLA Ops:
  0.6 32.4 %ladder.1 = (bf16[2,1,2,128,512]{4,3,2,1,0:T(8,128)(2,1)S(1)}, bf16[2,1,2,3584]{3,2,1,0:T(2,128)(2,1)S(1)}) custom-call(s32[2,16]{1,0:T(2,128)} %bitcast.6, s32[2,16]{1,0:T(2,128)} %bitcast.7, bf16[2,1,2,576]{3,2,1,0:T(2,128)(2,1)} %fresh_hbm.1, bf16[2,1,2,3584]{3,2,1,0:T(2,128)(2,1)} %hidden_hbm.1, s32[2,1,2,8]{3,2,1,0:T(2,128)} %routes_hbm.1, ...), custom_call_target="tpu_custom_call" | custom-call | tf_op jit(solution)/shard_map/ladder/pallas_call | solution.py:467
  33.1 0.8 %settle.1 = (bf16[2,1,2,128,512]{4,3,2,1,0:T(8,128)(2,1)}, bf16[2,1,2,3584]{3,2,1,0:T(2,128)(2,1)}) custom-call(bf16[2,1,2,128,512]{4,3,2,1,0:T(8,128)(2,1)S(1)} %get-tuple-element.4.attended_ref, bf16[2,1,2,3584]{3,2,1,0:T(2,128)(2,1)S(1)} %get-tuple-element.5.moe_ref), custom_call_target="tpu_custom_call" | custom-call | tf_op jit(solution)/shard_map/settle/pallas_call | solution.py:529

commit v7 on v6

--- a/solution.py
+++ b/solution.py
@@ -79,7 +79,11 @@
     cell = lax.rem(rank, 4)
     across_side, across_up = rank + 1 - 2 * side, rank + 2 - 4 * up
     diagonal = rank - cell + 3 - cell
-    plane = (diagonal, across_side, across_up)
+    plane = (
+        diagonal,
+        across_side * core + across_up * (1 - core),
+        across_up * core + across_side * (1 - core),
+    )
     other = 1 - core
     mine = core * half + cell
     far_rank = lax.rem(rank + ranks // 2, ranks)

time: 34 us -> 34 us (level)
  no operation moved by 1% of the time
where the time goes in v7:
time: 34 us; the launch traced here: 33.9 us
  Pallas kernels  33.2 us (98%)
  between operations  0.64 us (2%)
    pallas_call x1, Pallas kernels, ladder(): pl.pallas_call(functools.partial(ladder_kernel, dict(ranks=ranks, line=li...  32.4 us
    pallas_call x1, Pallas kernels, ladder(): pl.pallas_call(settle_kernel, out_shape=tuple((jax.ShapeDtypeStruct(one.s...  0.81 us

profile of v7, /device:TPU:0, one launch (start us, length us, event | category | flops | bytes accessed | tf_op | source)
XLA Modules:
  0.0 33.9 jit_solution(1019770680675210803)
XLA Ops:
  0.6 32.4 %ladder.1 = (bf16[2,1,2,128,512]{4,3,2,1,0:T(8,128)(2,1)S(1)}, bf16[2,1,2,3584]{3,2,1,0:T(2,128)(2,1)S(1)}) custom-call(s32[2,16]{1,0:T(2,128)} %bitcast.6, s32[2,16]{1,0:T(2,128)} %bitcast.7, bf16[2,1,2,576]{3,2,1,0:T(2,128)(2,1)} %fresh_hbm.1, bf16[2,1,2,3584]{3,2,1,0:T(2,128)(2,1)} %hidden_hbm.1, s32[2,1,2,8]{3,2,1,0:T(2,128)} %routes_hbm.1, ...), custom_call_target="tpu_custom_call" | custom-call | tf_op jit(solution)/shard_map/ladder/pallas_call | solution.py:471
  33.1 0.8 %settle.1 = (bf16[2,1,2,128,512]{4,3,2,1,0:T(8,128)(2,1)}, bf16[2,1,2,3584]{3,2,1,0:T(2,128)(2,1)}) custom-call(bf16[2,1,2,128,512]{4,3,2,1,0:T(8,128)(2,1)S(1)} %get-tuple-element.4.attended_ref, bf16[2,1,2,3584]{3,2,1,0:T(2,128)(2,1)S(1)} %get-tuple-element.5.moe_ref), custom_call_target="tpu_custom_call" | custom-call | tf_op jit(solution)/shard_map/settle/pallas_call | solution.py:533
